TPU v7x, 256 devices: a whole 4x4x8 slice. The times are simulated.
256 devices in a mesh: dp: 32 (over y_lo, z, core), proto: 8 (over x, y_hi).
Axes of the slice: x: 4, y: 4 (y_hi: 2, y_lo: 2; y = y_hi * 2 + y_lo), z: 8, core: 2. Of those that a mesh axis runs over, the one named last changes fastest.
Arguments:
- feature_matrix: bfloat16 [8192, 128], P('dp'), may hold values from -64 to 64
- tangent_embed: bfloat16 [8192, 128], P('dp'), may hold values from -2 to 2
- anchor_matrix: bfloat16 [65536, 128], P('proto'), may hold values from -4 to 4
- anchor_perturbation: bfloat16 [65536, 128], P('proto'), may hold values from -0.5 to 0.5
- codes: bfloat16 [8192, 65536], P('dp', 'proto'), may hold values from 0 to 3, as said below
- partner_lookup: int32 [8192], P('dp'), may hold values from 0 to 8191, as said below
Outputs:
- hvp_embed: bfloat16 [8192, 128], P('dp')
- hvp_proto: bfloat16 [65536, 128], P('proto')
Inputs may be any that keep to these rules, and one draw needn't show every extreme that they name: partner_lookup[partner_lookup[i]] = i and partner_lookup[i] != i for every crop i. `codes`: positive.
All inputs are finite; a program needn't handle non-finite values.
Results may differ from a plain program's by a relative error of at most 0.0051.
Values may be sent and summed in bfloat16 or wider, within the bound.
No kernel may reach another device: no remote copies, remote signals or barrier semaphores. Data moves between devices by JAX's collectives and lax.ppermute only.
A program may use at most 128 MiB of HBM per device.

v0:
```python
import jax
import jax.numpy as jnp
from jax import lax
from jax.sharding import PartitionSpec as P

softening_constant = 0.1


def aggregated_elements(left, right):
    return lax.dot_general(
        left, right, (((1,), (1,)), ((), ())), preferred_element_type=jnp.float32
    )


def reduce_along_samples(left, right):
    return lax.dot_general(
        left, right, (((0,), (0,)), ((), ())), preferred_element_type=jnp.float32
    )


def body(feature_matrix, tangent_embed, anchor_matrix, anchor_perturbation, codes, partner_lookup):
    collected_features, gathered_tan = (
        lax.all_gather(feature_matrix, "dp", axis=0, tiled=True),
        lax.all_gather(tangent_embed, "dp", axis=0, tiled=True),
    )
    traded_contributions = jnp.take(collected_features, partner_lookup, axis=0)
    swapped_tan = jnp.take(gathered_tan, partner_lookup, axis=0)
    unscaled_affinity = (
        aggregated_elements(traded_contributions, anchor_matrix) / softening_constant
    )
    similarity_direction = (
        aggregated_elements(swapped_tan, anchor_matrix)
        + aggregated_elements(traded_contributions, anchor_perturbation)
    ) / softening_constant
    local_max = jnp.max(unscaled_affinity, axis=1)
    local_mass = jnp.sum(codes, axis=1, dtype=jnp.float32)
    row_max = lax.pmax(local_max, "proto")
    exponent = jnp.exp(unscaled_affinity - row_max[:, None])
    softmax_total, weighted, line_sum_norm = lax.psum(
        (jnp.sum(exponent, axis=1), jnp.sum(exponent * similarity_direction, axis=1), local_mass),
        "proto",
    )
    model_likelihood = exponent / softmax_total[:, None]
    mean_code_vector = weighted / softmax_total
    outer_patch_multiplier = (
        softening_constant
        * line_sum_norm[:, None]
        * model_likelihood
        * (similarity_direction - mean_code_vector[:, None])
    ).astype(jnp.bfloat16)
    right_crop_factor = (
        softening_constant * (line_sum_norm[:, None] * model_likelihood - codes.astype(jnp.float32))
    ).astype(jnp.bfloat16)
    partial_embed = jnp.dot(
        outer_patch_multiplier, anchor_matrix, preferred_element_type=jnp.float32
    ) + jnp.dot(right_crop_factor, anchor_perturbation, preferred_element_type=jnp.float32)
    incomplete_anchor_grad = reduce_along_samples(
        outer_patch_multiplier, traded_contributions
    ) + reduce_along_samples(right_crop_factor, swapped_tan)
    hvp_proto = lax.psum(incomplete_anchor_grad, "dp").astype(jnp.bfloat16)
    summed = lax.psum(partial_embed, "proto").astype(jnp.bfloat16)
    gathered_out = lax.all_gather(summed, "dp", axis=0, tiled=True)
    hvp_embed = jnp.take(gathered_out, partner_lookup, axis=0)
    return (hvp_embed, hvp_proto)


def solution(mesh):
    in_specs = (
        P("dp", None),
        P("dp", None),
        P("proto", None),
        P("proto", None),
        P("dp", "proto"),
        P("dp"),
    )
    out_specs = (P("dp", None), P("proto", None))
    return jax.shard_map(body, mesh=mesh, in_specs=in_specs, out_specs=out_specs, check_vma=False)
```

profile of v0, /device:TPU:8, one launch (start us, length us, event | category | flops | bytes accessed | tf_op | source)
XLA Modules:
  0.0 401.0 jit_solution(2757636841518823086)
XLA Ops:
  7.2 0.7 all-gather.6.cloned.1.call-update
  8.0 0.7 all-gather.4.cloned.1.call-update
  8.7 0.0 all-gather.8.cloned.1.call-start
  8.7 0.7 compare_select_fusion
  9.4 0.7 compare_and_fusion
  10.1 2.8 convert_reduce_fusion
  12.9 63.6 %all-gather.6.cloned.1.call-done = bf16[8192,128]{1,0:T(8,128)(2,1)} async-done(((bf16[256,128]{1,0:T(8,128)(2,1)}), bf16[8192,128]{1,0:T(8,128)(2,1)}) %all-gather.6.cloned.1.call-update) | async-done | bytes 2097168 | tf_op jit(solution)/shard_map/all_gather | solution.py:24
  76.6 2.6 gather_fusion.1
  79.2 4.5 %fusion.5 = f32[256,8192]{1,0:T(8,128)} fusion(bf16[8192,128]{1,0:T(8,128)(2,1)S(1)} %copy-done, bf16[256,128]{1,0:T(8,128)(2,1)S(1)} %gather_fusion.1, pred[256]{0:T(512)(128)(4,1)S(1)} %compare_and_fusion), kind=kOutput, calls=%fused_computation.20 | convolution fusion | flops 536903680 | bytes 10551552 | tf_op jit(solution)/shard_map/dot_general | solution.py:10
  83.7 58.8 %all-gather.4.cloned.1.call-done = bf16[8192,128]{1,0:T(8,128)(2,1)} async-done(((bf16[256,128]{1,0:T(8,128)(2,1)}), bf16[8192,128]{1,0:T(8,128)(2,1)}) %all-gather.4.cloned.1.call-update) | async-done | bytes 2097168 | tf_op jit(solution)/shard_map/all_gather | solution.py:23
  142.5 2.6 gather_fusion
  145.1 4.5 %fusion.9 = (f32[256]{0:T(256)S(1)}, f32[256,8192]{1,0:T(8,128)}) fusion(bf16[8192,128]{1,0:T(8,128)(2,1)S(1)} %copy-done, bf16[256,128]{1,0:T(8,128)(2,1)S(1)} %gather_fusion, pred[256]{0:T(512)(128)(4,1)S(1)} %compare_and_fusion), kind=kOutput, calls=%fused_computation.28 | convolution fusion | flops 541097728 | bytes 10552576 | tf_op jit(solution)/shard_map/dot_general | solution.py:10
  149.6 23.3 %pmax.7 = f32[256]{0:T(256)S(1)} all-reduce(f32[256]{0:T(256)S(1)} %get-tuple-element.10), channel_id=1, replica_groups=mesh['dp'=32,'proto'=8] {'proto'}, use_global_device_ids=true, to_apply=%region_3.5 | all-reduce | flops 256 | bytes 2048 | tf_op jit(solution)/shard_map/pmax | solution.py:37
  172.8 10.1 %fusion.4 = (f32[256]{0:T(256)S(1)}, f32[256]{0:T(256)S(1)}, f32[256,8192]{1,0:T(8,128)}) fusion(f32[256,8192]{1,0:T(8,128)} %get-tuple-element.11, f32[256]{0:T(256)S(1)} %pmax.7, f32[256,8192]{1,0:T(8,128)} %fusion.5, bf16[8192,128]{1,0:T(8,128)(2,1)} %param.11, bf16[256,128]{1,0:T(8,128)(2,1)S(1)} %gather_fusion, pred[256]{0:T(512)(128)(4,1)S(1)} %compare_and_fusion), kind=kOutput, calls=%fused_computation.15 | convolution fusion | flops 549486080 | bytes 27331840 | tf_op jit(solution)/shard_map/dot_general | solution.py:10
  182.9 19.1 %all-reduce = (f32[256]{0:T(256)S(1)}, f32[256]{0:T(256)S(1)}, f32[256]{0:T(256)S(1)}) all-reduce(f32[256]{0:T(256)S(1)} %get-tuple-element.4, f32[256]{0:T(256)S(1)} %get-tuple-element.3, f32[256]{0:T(256)S(1)} %convert_reduce_fusion), channel_id=1, replica_groups=mesh['dp'=32,'proto'=8] {'proto'}, use_global_device_ids=true, to_apply=%region_7.9 | all-reduce | flops 768 | bytes 6144 | tf_op jit(solution)/shard_map/psum | solution.py:39
  202.1 9.7 %fusion.2 = (bf16[256,8192]{1,0:T(8,128)(2,1)S(1)}, bf16[256,8192]{1,0:T(8,128)(2,1)S(1)}) fusion(bf16[256,8192]{1,0:T(8,128)(2,1)} %param.12, f32[256]{0:T(256)S(1)} %get-tuple-element.7, f32[256]{0:T(256)S(1)} %get-tuple-element.6, f32[256,8192]{1,0:T(8,128)} %get-tuple-element.11, f32[256]{0:T(256)S(1)} %pmax.7, f32[256,8192]{1,0:T(8,128)} %get-tuple-element.12, ...), kind=kLoop, calls=%fused_computation.10 | loop fusion | flops 23068672 | bytes 29365248 | tf_op jit(solution)/shard_map/convert_element_type | solution.py:53
  211.7 1.3 fusion.10
  213.0 1.4 fusion.8
  214.4 3.4 convolution_add_fusion.1
  217.8 1.4 convolution_add_fusion.2
  219.1 41.8 %all-reduce.3 = bf16[256,128]{1,0:T(8,128)(2,1)} all-reduce(f32[256,128]{1,0:T(8,128)S(1)} %convolution_add_fusion.2), channel_id=1, replica_groups=mesh['dp'=32,'proto'=8] {'proto'}, use_global_device_ids=true, to_apply=%region_8.10 | all-reduce | flops 32768 | bytes 196608 | tf_op jit(solution)/shard_map/psum | solution.py:61
  261.0 130.1 %all-reduce.4 = bf16[8192,128]{1,0:T(8,128)(2,1)} all-reduce(f32[8192,128]{1,0:T(8,128)} %convolution_add_fusion.1), channel_id=1, replica_groups=mesh['dp'=32,'proto'=8] {'dp'}, use_global_device_ids=true, to_apply=%region_9.11 | all-reduce | flops 1048576 | bytes 6291456 | tf_op jit(solution)/shard_map/psum | solution.py:60
  391.1 2.6 gather_fusion.2
  393.7 0.7 broadcast_select_fusion.2
  (11 shorter events, 0.1 us)
Async XLA Ops:
  7.2 72.0 %copy-start = (bf16[8192,128]{1,0:T(8,128)(2,1)S(1)}, bf16[8192,128]{1,0:T(8,128)(2,1)}, u32[]{:S(2)}) copy-start(bf16[8192,128]{1,0:T(8,128)(2,1)} %param.10) | copy-start | bytes 6291460
  7.2 69.4 %all-gather.6.cloned.1.call-start = ((), (), s32[]{:S(2)}) async-start(), calls=%async_computation.1 | async-start | bytes 2162688 | tf_op jit(solution)/shard_map/all_gather | solution.py:24
  7.9 134.6 %all-gather.4.cloned.1.call-start = ((), (), s32[]{:S(2)}) async-start(), calls=%async_computation | async-start | bytes 2162688 | tf_op jit(solution)/shard_map/all_gather | solution.py:23
  8.7 382.5 %all-gather.8.cloned.1.call-start = ((), (), s32[]{:S(2)}) async-start(), calls=%async_computation.2 | async-start | bytes 2162688 | tf_op jit(solution)/shard_map/all_gather | solution.py:62
  214.4 3.4 copy-start.1
Sparse Core Ops, SparseCore 0:
  9.8 66.6 all-gather.5
  78.4 63.9 all-gather.3
  261.1 60.5 all-gather.7
where the time goes:
time: 401 us
  blocking collectives  214 us (53%)
  waiting for transfers between devices  124 us (31%)
  matrix products  26.5 us (7%)
  other arithmetic  14.6 us (4%)
  between operations  13.8 us (3%)
  local copies, waits for them, and re-layouts  7.78 us (2%)
    psum x1, blocking collectives, body(): hvp_proto = lax.psum(incomplete_anchor_grad, 'dp').astype(jnp.bfloat16)  130 us
    all_gather x1, waiting for transfers between devices, body(): lax.all_gather(tangent_embed, 'dp', axis=0, tiled=True)  63.6 us
    all_gather x1, waiting for transfers between devices, body(): lax.all_gather(feature_matrix, 'dp', axis=0, tiled=True)  58.8 us
    psum x1, blocking collectives, body(): summed = lax.psum(partial_embed, 'proto').astype(jnp.bfloat16)  41.8 us
    pmax x1, blocking collectives, body(): row_max = lax.pmax(local_max, 'proto')  23.3 us
    dot_general x3, matrix products, aggregated_elements(): lax.dot_general(left, right, (((1,), (1,)), ((), ())), preferred_element_...  19.1 us
    psum x1, blocking collectives, body(): lax.psum((jnp.sum(exponent, axis=1), jnp.sum(exponent * similarity_direct...  19.1 us
    convert_element_type x1, other arithmetic, body(): right_crop_factor = (softening_constant * (line_sum_norm[:, None] * model...  9.65 us
  transfers between devices with their start and end apart: 3, of which 2 were waited for; matrix products, arithmetic and copies ran while one was open for 3% of the time, Pallas kernels for 0%

commit v1 on v0

--- a/solution.py
+++ b/solution.py
@@ -1,9 +1,22 @@
+import functools
 import jax
 import jax.numpy as jnp
 from jax import lax
 from jax.sharding import PartitionSpec as P
 
 softening_constant = 0.1
+
+
+def compute_the_ports(xs, d0):
+    return jnp.concatenate(
+        lax.all_to_all(
+            jnp.stack(lax.axis_size("dp") * [xs]), split_axis=0, axis_name="dp", concat_axis=0
+        ),
+        axis=d0,
+    )
+
+
+play_rounds = functools.partial(compute_the_ports, d0=0)
 
 
 def aggregated_elements(left, right):
@@ -20,7 +33,7 @@
 
 def body(feature_matrix, tangent_embed, anchor_matrix, anchor_perturbation, codes, partner_lookup):
     collected_features, gathered_tan = (
-        lax.all_gather(feature_matrix, "dp", axis=0, tiled=True),
+        play_rounds(feature_matrix),
         lax.all_gather(tangent_embed, "dp", axis=0, tiled=True),
     )
     traded_contributions = jnp.take(collected_features, partner_lookup, axis=0)

time: 401 us -> 360 us (0.90)
  waiting for transfers between devices: 124 us -> 69.9 us
  starting transfers between devices: 0.11 us -> 10.2 us
    all_gather x1 -> x0, waiting for transfers between devices: 58.8 us -> none  [body(): lax.all_gather(feature_matrix, 'dp', axis=0, tiled=True)]
    all_to_all x0 -> x1, waiting for transfers between devices: none -> 51.6 us  [compute_the_ports(): lax.all_to_all(jnp.stack(lax.axis_size('dp') * [xs]), split_axis=0, axis_...]
    all_gather x1, waiting for transfers between devices: 63.6 us -> 17.6 us  [body(): lax.all_gather(tangent_embed, 'dp', axis=0, tiled=True)]
    all_to_all x0 -> x1, starting transfers between devices: none -> 10.1 us  [compute_the_ports(): lax.all_to_all(jnp.stack(lax.axis_size('dp') * [xs]), split_axis=0, axis_...]
  transfers between devices with their start and end apart: 3 -> 3, of which waited for: 2 -> 2; matrix products, arithmetic and copies ran while one was open for 3% -> 2% of each run, Pallas kernels for 0% -> 0%
where the time goes in v1:
time: 360 us
  blocking collectives  215 us (60%)
  waiting for transfers between devices  69.9 us (19%)
  matrix products  26.5 us (7%)
  between operations  14.1 us (4%)
  other arithmetic  13.3 us (4%)
  local copies, waits for them, and re-layouts  10.6 us (3%)
  starting transfers between devices  10.2 us (3%)
    psum x1, blocking collectives, body(): hvp_proto = lax.psum(incomplete_anchor_grad, 'dp').astype(jnp.bfloat16)  130 us
    all_to_all x1, waiting for transfers between devices, compute_the_ports(): lax.all_to_all(jnp.stack(lax.axis_size('dp') * [xs]), split_axis=0, axis_...  51.6 us
    psum x1, blocking collectives, body(): summed = lax.psum(partial_embed, 'proto').astype(jnp.bfloat16)  41.8 us
    pmax x1, blocking collectives, body(): row_max = lax.pmax(local_max, 'proto')  24.2 us
    dot_general x3, matrix products, aggregated_elements(): lax.dot_general(left, right, (((1,), (1,)), ((), ())), preferred_element_...  19.1 us
    psum x1, blocking collectives, body(): lax.psum((jnp.sum(exponent, axis=1), jnp.sum(exponent * similarity_direct...  19.1 us
    all_gather x1, waiting for transfers between devices, body(): lax.all_gather(tangent_embed, 'dp', axis=0, tiled=True)  17.6 us
    all_to_all x1, starting transfers between devices, compute_the_ports(): lax.all_to_all(jnp.stack(lax.axis_size('dp') * [xs]), split_axis=0, axis_...  10.1 us
  transfers between devices with their start and end apart: 3, of which 2 were waited for; matrix products, arithmetic and copies ran while one was open for 2% of the time, Pallas kernels for 0%

profile of v1, /device:TPU:8, one launch (start us, length us, event | category | flops | bytes accessed | tf_op | source)
XLA Modules:
  0.0 360.1 jit_solution(10838420740806797036)
XLA Ops:
  7.2 2.8 stack.2
  10.0 10.1 %all-to-all-start = ((bf16[32,256,128]{2,1,0:T(8,128)(2,1)}), bf16[32,256,128]{2,1,0:T(8,128)(2,1)}, u32[]{:S(2)}, u32[]{:S(2)}) async-start(bf16[32,256,128]{2,1,0:T(8,128)(2,1)} %stack.2), calls=%async_computation | async-start | bytes 4194304 | tf_op jit(solution)/shard_map/all_to_all | solution.py:12
  20.1 0.0 all-gather.3.cloned.1.call-start
  20.2 0.7 all-gather.3.cloned.1.call-update
  20.9 0.0 all-gather.5.cloned.1.call-start
  21.0 2.8 convert_reduce_fusion
  23.8 51.6 %all-to-all-done = bf16[32,256,128]{2,1,0:T(8,128)(2,1)} async-done(((bf16[32,256,128]{2,1,0:T(8,128)(2,1)}), bf16[32,256,128]{2,1,0:T(8,128)(2,1)}, u32[]{:S(2)}, u32[]{:S(2)}) %all-to-all-start) | async-done | bytes 2097184 | tf_op jit(solution)/shard_map/all_to_all | solution.py:12
  75.4 2.6 gather_fusion
  78.0 17.6 %all-gather.3.cloned.1.call-done = bf16[8192,128]{1,0:T(8,128)(2,1)} async-done(((bf16[256,128]{1,0:T(8,128)(2,1)}), bf16[8192,128]{1,0:T(8,128)(2,1)}) %all-gather.3.cloned.1.call-update) | async-done | bytes 2097168 | tf_op jit(solution)/shard_map/all_gather | solution.py:37
  95.7 2.6 gather_fusion.1
  98.2 4.5 %fusion.5 = f32[256,8192]{1,0:T(8,128)} fusion(bf16[8192,128]{1,0:T(8,128)(2,1)S(1)} %copy-done, bf16[256,128]{1,0:T(8,128)(2,1)S(1)} %gather_fusion.1, pred[256]{0:T(512)(128)(4,1)S(1)} %compare_and_fusion), kind=kOutput, calls=%fused_computation.20 | convolution fusion | flops 536903680 | bytes 10551552 | tf_op jit(solution)/shard_map/dot_general | solution.py:23
  102.7 4.5 %fusion.9 = (f32[256]{0:T(256)S(1)}, f32[256,8192]{1,0:T(8,128)}) fusion(bf16[8192,128]{1,0:T(8,128)(2,1)S(1)} %copy-done, bf16[256,128]{1,0:T(8,128)(2,1)S(1)} %gather_fusion, pred[256]{0:T(512)(128)(4,1)S(1)} %compare_and_fusion), kind=kOutput, calls=%fused_computation.28 | convolution fusion | flops 541097728 | bytes 10552576 | tf_op jit(solution)/shard_map/dot_general | solution.py:23
  107.3 24.2 %pmax.7 = f32[256]{0:T(256)S(1)} all-reduce(f32[256]{0:T(256)S(1)} %get-tuple-element.10), channel_id=1, replica_groups=mesh['dp'=32,'proto'=8] {'proto'}, use_global_device_ids=true, to_apply=%region_3.5 | all-reduce | flops 256 | bytes 2048 | tf_op jit(solution)/shard_map/pmax | solution.py:50
  131.5 10.1 %fusion.4 = (f32[256]{0:T(256)S(1)}, f32[256]{0:T(256)S(1)}, f32[256,8192]{1,0:T(8,128)}) fusion(f32[256,8192]{1,0:T(8,128)} %get-tuple-element.11, f32[256]{0:T(256)S(1)} %pmax.7, f32[256,8192]{1,0:T(8,128)} %fusion.5, bf16[8192,128]{1,0:T(8,128)(2,1)} %param.11, bf16[256,128]{1,0:T(8,128)(2,1)S(1)} %gather_fusion, pred[256]{0:T(512)(128)(4,1)S(1)} %compare_and_fusion), kind=kOutput, calls=%fused_computation.15 | convolution fusion | flops 549486080 | bytes 27331840 | tf_op jit(solution)/shard_map/dot_general | solution.py:23
  141.6 19.1 %all-reduce = (f32[256]{0:T(256)S(1)}, f32[256]{0:T(256)S(1)}, f32[256]{0:T(256)S(1)}) all-reduce(f32[256]{0:T(256)S(1)} %get-tuple-element.4, f32[256]{0:T(256)S(1)} %get-tuple-element.3, f32[256]{0:T(256)S(1)} %convert_reduce_fusion), channel_id=1, replica_groups=mesh['dp'=32,'proto'=8] {'proto'}, use_global_device_ids=true, to_apply=%region_7.9 | all-reduce | flops 768 | bytes 6144 | tf_op jit(solution)/shard_map/psum | solution.py:52
  160.7 9.7 %fusion.2 = (bf16[256,8192]{1,0:T(8,128)(2,1)S(1)}, bf16[256,8192]{1,0:T(8,128)(2,1)S(1)}) fusion(bf16[256,8192]{1,0:T(8,128)(2,1)} %param.12, f32[256]{0:T(256)S(1)} %get-tuple-element.7, f32[256]{0:T(256)S(1)} %get-tuple-element.6, f32[256,8192]{1,0:T(8,128)} %get-tuple-element.11, f32[256]{0:T(256)S(1)} %pmax.7, f32[256,8192]{1,0:T(8,128)} %get-tuple-element.12, ...), kind=kLoop, calls=%fused_computation.10 | loop fusion | flops 23068672 | bytes 29365248 | tf_op jit(solution)/shard_map/convert_element_type | solution.py:66
  170.4 1.3 fusion.10
  171.7 1.4 fusion.8
  173.0 3.4 convolution_add_fusion.1
  176.4 1.4 convolution_add_fusion.2
  177.8 41.8 %all-reduce.3 = bf16[256,128]{1,0:T(8,128)(2,1)} all-reduce(f32[256,128]{1,0:T(8,128)S(1)} %convolution_add_fusion.2), channel_id=1, replica_groups=mesh['dp'=32,'proto'=8] {'proto'}, use_global_device_ids=true, to_apply=%region_8.10 | all-reduce | flops 32768 | bytes 196608 | tf_op jit(solution)/shard_map/psum | solution.py:74
  219.7 130.2 %all-reduce.4 = bf16[8192,128]{1,0:T(8,128)(2,1)} all-reduce(f32[8192,128]{1,0:T(8,128)} %convolution_add_fusion.1), channel_id=1, replica_groups=mesh['dp'=32,'proto'=8] {'dp'}, use_global_device_ids=true, to_apply=%region_9.11 | all-reduce | flops 1048576 | bytes 6291456 | tf_op jit(solution)/shard_map/psum | solution.py:73
  349.9 2.6 gather_fusion.2
  352.5 0.7 broadcast_select_fusion.2
  (13 shorter events, 0.1 us)
Async XLA Ops:
  7.2 91.1 %copy-start = (bf16[8192,128]{1,0:T(8,128)(2,1)S(1)}, bf16[8192,128]{1,0:T(8,128)(2,1)}, u32[]{:S(2)}) copy-start(bf16[8192,128]{1,0:T(8,128)(2,1)} %param.10) | copy-start | bytes 6291460
  7.2 13.7 %copy-start.2 = (s32[256]{0:T(256)S(1)}, s32[256]{0:T(256)}, u32[]{:S(2)}) copy-start(s32[256]{0:T(256)} %param.13) | copy-start | bytes 3076
  10.0 65.5 %all-to-all-start = ((bf16[32,256,128]{2,1,0:T(8,128)(2,1)}), bf16[32,256,128]{2,1,0:T(8,128)(2,1)}, u32[]{:S(2)}, u32[]{:S(2)}) async-start(bf16[32,256,128]{2,1,0:T(8,128)(2,1)} %stack.2), calls=%async_computation | async-start | bytes 4194304 | tf_op jit(solution)/shard_map/all_to_all | solution.py:12
  20.1 75.5 %all-gather.3.cloned.1.call-start = ((), (), s32[]{:S(2)}) async-start(), calls=%async_computation.1 | async-start | bytes 2162688 | tf_op jit(solution)/shard_map/all_gather | solution.py:37
  20.9 329.0 %all-gather.5.cloned.1.call-start = ((), (), s32[]{:S(2)}) async-start(), calls=%async_computation.2 | async-start | bytes 2162688 | tf_op jit(solution)/shard_map/all_gather | solution.py:75
  173.0 3.4 copy-start.1
Sparse Core Ops, SparseCore 0:
  22.8 72.8 all-gather.2
  219.8 60.5 all-gather.4
